TPU v7x, 512 devices: a whole 4x4x16 slice. The times are simulated.
512 devices in a mesh: gz: 32 (over z_lo, y), row: 16 (over z_hi, x, core).
Axes of the slice: x: 4, y: 4, z: 16 (z_hi: 2, z_lo: 8; z = z_hi * 8 + z_lo), core: 2. Of those that a mesh axis runs over, the one named last changes fastest.
Arguments:
- density: float32 [256, 128, 256], P('gz', 'row'), may hold values from 0.3 to 3
- pressure: float32 [256, 128, 256], P('gz', 'row'), may hold values from 0.3 to 3
- velocity: float32 [3, 256, 128, 256], P(None, 'gz', 'row'), may hold values from -3 to 3
- boundary: int32 [6], replicated, may hold values from 0 to 1
Outputs:
- density_out: float32 [256, 128, 256], P('gz', 'row')
- pressure_out: float32 [256, 128, 256], P('gz', 'row')
- velocity_out: float32 [3, 256, 128, 256], P(None, 'gz', 'row')
Inputs may be any that keep to these rules, and one draw needn't show every extreme that they name: `boundary`: 1 marks a reflecting face, 0 an outflow face; entries 2k and 2k+1 are the lower and upper faces of x, y, z in turn.
All inputs are finite; a program needn't handle non-finite values.
Results may differ from a plain program's by a relative error of at most 0.0003.
Values sent between devices are 32-bit elements; how exact they have to be, the bound alone decides.
No kernel may reach another device: no remote copies, remote signals or barrier semaphores. Data moves between devices by JAX's collectives and lax.ppermute only.
A program may use at most 64 MiB of HBM per device.

v0:
```python
import jax
import jax.numpy as jnp
import numpy as np
from jax import lax
from jax.sharding import PartitionSpec as P

RIEMANN_ITERS = 4
gamma_gas = 1.4
courant_ratio = 0.05
dens_floor = 0.02
press_floor = 0.02
star_frac = 0.1


def padded_2(cells, sides, width):
    for axis, dim in sides:
        count = lax.axis_size(axis)
        ends = count - 1
        head = lax.slice_in_dim(cells, 0, width, axis=dim)
        tail = lax.slice_in_dim(cells, cells.shape[dim] - width, cells.shape[dim], axis=dim)
        cells = jnp.concatenate(
            [
                lax.ppermute(tail, axis, [(i, (i + 1) % count) for i in range(ends)]),
                cells,
                lax.ppermute(head, axis, [((i + 1) % count, i) for i in range(ends)]),
            ],
            axis=dim,
        )
    return cells


def mirror_sign(normal, ndim):
    table = np.ones(5, np.float32)
    table[normal] = -1.0
    return jnp.asarray(table.reshape((5,) + (1,) * (ndim - 1)))


def normal_mask(normal, ndim):
    table = np.zeros(3, np.float32)
    table[normal - 2] = 1.0
    return jnp.asarray(table.reshape((3,) + (1,) * (ndim - 1)))


def boundary_cells(interior, along, face_flag, at_lower, normal):
    reflect = jnp.flip(interior, axis=along) * mirror_sign(normal, interior.ndim)
    edge_index = 0 if at_lower else 2
    edge_cell = lax.slice_in_dim(interior, edge_index, edge_index + 1, axis=along)
    outflow = jnp.concatenate([edge_cell, edge_cell, edge_cell], axis=along)
    return jnp.where(face_flag == 1, reflect, outflow)


def add_ghosts(fields, along, low_flag, high_flag, normal):
    inner_len = fields.shape[along]
    lower_ghosts = boundary_cells(
        lax.slice_in_dim(fields, 0, 3, axis=along), along, low_flag, True, normal
    )
    upper_ghosts = boundary_cells(
        lax.slice_in_dim(fields, inner_len - 3, inner_len, axis=along),
        along,
        high_flag,
        False,
        normal,
    )
    return jnp.concatenate([lower_ghosts, fields, upper_ghosts], axis=along)


def fix_edges(padded, along, low_flag, high_flag, at_first, at_last, normal):
    padded_len = padded.shape[along]
    lower_ghosts = boundary_cells(
        lax.slice_in_dim(padded, 3, 6, axis=along), along, low_flag, True, normal
    )
    upper_ghosts = boundary_cells(
        lax.slice_in_dim(padded, padded_len - 6, padded_len - 3, axis=along),
        along,
        high_flag,
        False,
        normal,
    )
    lower_ghosts = jnp.where(at_first, lower_ghosts, lax.slice_in_dim(padded, 0, 3, axis=along))
    upper_ghosts = jnp.where(
        at_last, upper_ghosts, lax.slice_in_dim(padded, padded_len - 3, padded_len, axis=along)
    )
    middle = lax.slice_in_dim(padded, 3, padded_len - 3, axis=along)
    return jnp.concatenate([lower_ghosts, middle, upper_ghosts], axis=along)


def conserved(prims):
    dens = prims[0:1]
    speeds = prims[2:5]
    energy = prims[1:2] / (gamma_gas - 1.0) + 0.5 * dens * jnp.sum(
        speeds * speeds, axis=0, keepdims=True
    )
    return jnp.concatenate([dens, energy, dens * speeds], axis=0)


def primitive(conserv):
    dens = jnp.maximum(conserv[0:1], dens_floor)
    speeds = conserv[2:5] / dens
    press = (gamma_gas - 1.0) * (
        conserv[1:2] - 0.5 * dens * jnp.sum(speeds * speeds, axis=0, keepdims=True)
    )
    return jnp.concatenate([dens, jnp.maximum(press, press_floor), speeds], axis=0)


def shock_side(star_press, side_press, sound_imp):
    ratio_g = (gamma_gas + 1.0) / (2.0 * gamma_gas)
    wave_speed = sound_imp * jnp.sqrt(1.0 + ratio_g * (star_press / side_press - 1.0))
    jump_speed = (star_press - side_press) / wave_speed
    jump_slope = (
        sound_imp
        * sound_imp
        * (1.0 + ratio_g * (star_press - side_press) / (2.0 * side_press))
        / wave_speed**3
    )
    return (jump_speed, jump_slope)


def godunov(left_state, right_state, normal):
    dens_left, dens_right = (left_state[0], right_state[0])
    press_left, press_right = (left_state[1], right_state[1])
    normal_left, normal_right = (left_state[normal], right_state[normal])
    sound_left = jnp.sqrt(gamma_gas * press_left * dens_left)
    sound_right = jnp.sqrt(gamma_gas * press_right * dens_right)
    floor_press = star_frac * jnp.minimum(press_left, press_right)
    star_press = (
        sound_right * press_left
        + sound_left * press_right
        - sound_left * sound_right * (normal_right - normal_left)
    ) / (sound_left + sound_right)
    star_press = jnp.maximum(star_press, floor_press)
    for attempt in range(RIEMANN_ITERS):
        jump_left, slope_left = shock_side(star_press, press_left, sound_left)
        jump_right, slope_right = shock_side(star_press, press_right, sound_right)
        star_press = star_press - (normal_right - normal_left + jump_left + jump_right) / (
            slope_left + slope_right
        )
        star_press = jnp.maximum(star_press, floor_press)
    jump_left, slope_left = shock_side(star_press, press_left, sound_left)
    jump_right, slope_right = shock_side(star_press, press_right, sound_right)
    star_speed = 0.5 * (normal_left - jump_left + (normal_right + jump_right))
    upwind = star_speed > 0.0
    dens_up = jnp.where(upwind, dens_left, dens_right)
    press_up = jnp.where(upwind, press_left, press_right)
    selector = normal_mask(normal, left_state.ndim)
    vel_up = jnp.where(upwind[None], left_state[2:5], right_state[2:5])
    vel_up = selector * star_speed[None] + (1.0 - selector) * vel_up
    energy_up = press_up / (gamma_gas - 1.0) + 0.5 * dens_up * jnp.sum(vel_up * vel_up, axis=0)
    mass_flux = dens_up * star_speed
    energy_flux = (energy_up + star_press) * star_speed
    moment_flux = mass_flux[None] * vel_up + selector * star_press[None]
    return jnp.concatenate([mass_flux[None], energy_flux[None], moment_flux], axis=0)


def sweep_cells(padded, along, normal):
    inner_len = padded.shape[along] - 6

    def window(start, length):
        return lax.slice_in_dim(padded, start, start + length, axis=along)

    left_in = window(1, inner_len + 3)
    right_in = window(2, inner_len + 3)
    interfaces = (
        7.0 * (left_in + right_in) - (window(0, inner_len + 3) + window(3, inner_len + 3))
    ) / 12.0
    interfaces = jnp.clip(
        interfaces, jnp.minimum(left_in, right_in), jnp.maximum(left_in, right_in)
    )
    centres = window(2, inner_len + 2)
    to_left = lax.slice_in_dim(interfaces, 0, inner_len + 2, axis=along) - centres
    to_right = lax.slice_in_dim(interfaces, 1, inner_len + 3, axis=along) - centres
    west_edge = centres + jnp.clip(to_left, -2.0 * jnp.abs(to_right), 2.0 * jnp.abs(to_right))
    east_edge = centres + jnp.clip(to_right, -2.0 * jnp.abs(to_left), 2.0 * jnp.abs(to_left))
    left_state = lax.slice_in_dim(east_edge, 0, inner_len + 1, axis=along)
    right_state = lax.slice_in_dim(west_edge, 1, inner_len + 2, axis=along)
    fluxes = godunov(left_state, right_state, normal)
    conserv = conserved(window(3, inner_len))
    conserv = conserv - courant_ratio * (
        lax.slice_in_dim(fluxes, 1, inner_len + 1, axis=along)
        - lax.slice_in_dim(fluxes, 0, inner_len, axis=along)
    )
    return primitive(conserv)


def z_sweep(fields, boundary):
    padded = padded_2(fields, (("gz", 1),), 3)
    at_first = lax.axis_index("gz") == 0
    at_last = lax.axis_index("gz") == lax.axis_size("gz") - 1
    padded = fix_edges(padded, 1, boundary[4], boundary[5], at_first, at_last, 4)
    return sweep_cells(padded, 1, 4)


def return_rows(fields):
    return lax.all_to_all(fields, "row", split_axis=2, concat_axis=3, tiled=True)


def on_device(density, pressure, velocity, boundary):
    fields = jnp.concatenate([density[None], pressure[None], velocity], axis=0)
    fields = sweep_cells(add_ghosts(fields, 3, boundary[0], boundary[1], 2), 3, 2)
    turned = jnp.swapaxes(
        lax.all_to_all(fields, "row", split_axis=3, concat_axis=2, tiled=True), 2, 3
    )
    columns = sweep_cells(add_ghosts(turned, 3, boundary[2], boundary[3], 3), 3, 3)
    fields = z_sweep(return_rows(jnp.swapaxes(columns, 2, 3)), boundary)
    return (fields[0], fields[1], fields[2:5])


def solution(mesh):
    in_specs = (P("gz", "row", None), P("gz", "row", None), P(None, "gz", "row", None), P())
    out_specs = (P("gz", "row", None), P("gz", "row", None), P(None, "gz", "row", None))
    return jax.shard_map(
        on_device, mesh=mesh, in_specs=in_specs, out_specs=out_specs, check_vma=False
    )
```

profile of v0, /device:TPU:24, one launch (start us, length us, event | category | flops | bytes accessed | tf_op | source)
XLA Modules:
  0.0 135.5 jit_solution(8363824731809600280)
XLA Ops:
  0.7 1.1 fusion.16
  2.0 1.0 multiply_reduce_fusion.8
  3.1 0.3 copy.199
  3.3 0.6 fusion.144
  4.0 0.3 copy.200
  6.1 0.5 fusion.7
  6.6 0.3 minimum_add_fusion.3
  6.9 1.2 fusion.132
  8.9 3.1 %copy.187 = f32[5,8,8,256]{2,1,0,3:T(8,128)} copy(f32[5,8,8,256]{3,2,1,0:T(8,128)S(1)} %pad_maximum_fusion.8) | data formatting | bytes 655360 | tf_op jit(solution)/shard_map/concatenate | solution.py:102
  12.0 5.3 %reshape.81 = f32[16,1,5120]{2,1,0:T(1,128)} reshape(f32[256,5,8,8]{3,2,1,0:T(8,128)} %bitcast.119) | data formatting | bytes 655360
  17.3 17.7 %all-to-all-start = ((f32[16,1,5120]{2,1,0:T(1,128)}), f32[16,1,5120]{2,1,0:T(1,128)S(1)}, u32[]{:S(2)}, u32[]{:S(2)}) async-start(f32[16,1,5120]{2,1,0:T(1,128)} %reshape.81), calls=%async_computation | async-start | bytes 655360 | tf_op jit(solution)/shard_map/all_to_all | solution.py:200
  36.2 16.7 %all-to-all-done = f32[16,1,5120]{2,1,0:T(1,128)S(1)} async-done(((f32[16,1,5120]{2,1,0:T(1,128)}), f32[16,1,5120]{2,1,0:T(1,128)S(1)}, u32[]{:S(2)}, u32[]{:S(2)}) %all-to-all-start) | async-done | bytes 327712 | tf_op jit(solution)/shard_map/all_to_all | solution.py:200
  52.9 0.5 broadcast.1082
  53.4 1.4 %reduce.5 = f32[16,5120]{1,0:T(8,128)S(1)} reduce(f32[16,1,5120]{2,1,0:T(1,128)S(1)} %all-to-all-done, f32[]{:T(128)} %broadcast.1082), dimensions={1}, to_apply=%all_to_all.26.reduce_sub_computation | reduce | bytes 655364 | tf_op jit(solution)/shard_map/all_to_all | solution.py:200
  54.9 4.4 %reshape.82 = f32[256,5,8,8]{3,2,1,0:T(8,128)} reshape(f32[16,5120]{1,0:T(8,128)S(1)} %reduce.5) | data formatting | bytes 655360
  59.3 4.2 %copy.188 = f32[5,8,8,16,16]{4,2,3,1,0:T(8,128)S(1)} copy(f32[5,8,8,16,16]{2,1,0,4,3:T(8,128)} %bitcast.120) | data formatting | bytes 655360 | tf_op jit(solution)/shard_map/all_to_all | solution.py:200
  63.4 0.7 copy.189
  64.3 0.3 slice_reduce_fusion.1
  65.0 0.3 multiply_select_fusion.1
  65.3 0.3 pad_maximum_fusion
  65.6 0.6 fusion.3
  66.2 0.4 minimum_add_fusion.1
  66.7 1.6 %fusion.131 = (pred[8,16,129]{2,1,0:T(8,128)(4,1)S(1)}, f32[1,8,16,129]{3,2,1,0:T(8,128)S(1)}, f32[1,8,16,129]{3,2,1,0:T(8,128)S(1)}) fusion(f32[5,8,16,130]{3,2,1,0:T(8,128)S(1)} %get-tuple-element.33, f32[5,8,16,130]{3,2,1,0:T(8,128)S(1)} %get-tuple-element.32), kind=kLoop, calls=%fused_computation.271 | loop fusion | flops 2889600 | bytes 544896 | tf_op jit(solution)/shard_map/jit(_where)/broadcast_in_dim | solution.py:145
  69.1 0.8 copy.190
  70.0 1.7 %reshape.83 = f32[16,1,5120]{2,1,0:T(1,128)} reshape(f32[128,5,8,16]{3,2,1,0:T(8,128)S(1)} %bitcast.123) | data formatting | bytes 655360
  71.6 3.8 %all-to-all-start.1 = ((f32[16,1,5120]{2,1,0:T(1,128)}), f32[16,1,5120]{2,1,0:T(1,128)S(1)}, u32[]{:S(2)}, u32[]{:S(2)}) async-start(f32[16,1,5120]{2,1,0:T(1,128)} %reshape.83), calls=%async_computation.1 | async-start | bytes 655360 | tf_op jit(solution)/shard_map/all_to_all | solution.py:193
  76.6 16.0 %all-to-all-done.1 = f32[16,1,5120]{2,1,0:T(1,128)S(1)} async-done(((f32[16,1,5120]{2,1,0:T(1,128)}), f32[16,1,5120]{2,1,0:T(1,128)S(1)}, u32[]{:S(2)}, u32[]{:S(2)}) %all-to-all-start.1) | async-done | bytes 327712 | tf_op jit(solution)/shard_map/all_to_all | solution.py:193
  92.6 1.4 %reduce.6 = f32[16,5120]{1,0:T(8,128)S(1)} reduce(f32[16,1,5120]{2,1,0:T(1,128)S(1)} %all-to-all-done.1, f32[]{:T(128)} %broadcast.1082), dimensions={1}, to_apply=%all_to_all.30.reduce_sub_computation | reduce | bytes 655364 | tf_op jit(solution)/shard_map/all_to_all | solution.py:193
  94.0 0.9 reshape.84
  94.9 0.5 copy.202
  95.4 2.2 %multiply_reduce_fusion = (f32[8,8,16,16]{3,1,2,0:T(8,128)}, f32[3,8,8,16,16]{4,2,3,1,0:T(8,128)}) fusion(f32[5,8,8,16,16]{4,2,3,1,0:T(8,128)S(1)} %bitcast.121), kind=kLoop, calls=%fused_computation.1 | loop fusion | flops 81920 | bytes 458752 | tf_op jit(solution)/shard_map/reduce_sum | solution.py:90
  97.6 0.9 slice_multiply_fusion
  98.6 0.9 mul.1862
  99.7 3.0 %copy.197 = f32[5,8,8,16,16]{4,3,2,1,0:T(8,128)} copy(f32[5,8,8,16,16]{4,1,0,2,3:T(8,128)S(1)} %bitcast.118) | data formatting | bytes 655360 | tf_op jit(solution)/shard_map/all_to_all | solution.py:193
  102.7 2.7 %all_to_all.33 = f32[5,8,8,256]{3,2,1,0:T(8,128)S(1)} reshape(f32[5,8,8,16,16]{4,3,2,1,0:T(8,128)} %copy.197) | data formatting | bytes 655360 | tf_op jit(solution)/shard_map/all_to_all | solution.py:193
  105.5 0.7 fusion.139
  106.2 15.8 %collective-permute-start = (f32[5,3,8,256]{3,2,1,0:T(8,128)}, f32[5,3,8,256]{3,2,1,0:T(8,128)}, u32[]{:S(2)}, u32[]{:S(2)}) collective-permute-start(f32[5,3,8,256]{3,2,1,0:T(8,128)} %get-tuple-element.44), channel_id=1, source_target_pairs={{0,16},{16,32},{32,48},{48,64},{64,80},{80,96},{96,112},{112,128},... | collective-permute-start | bytes 368648 | tf_op jit(solution)/shard_map/ppermute | solution.py:23
  122.0 1.9 %collective-permute-start.1 = (f32[5,3,8,256]{3,2,1,0:T(8,128)}, f32[5,3,8,256]{3,2,1,0:T(8,128)}, u32[]{:S(2)}, u32[]{:S(2)}) collective-permute-start(f32[5,3,8,256]{3,2,1,0:T(8,128)} %get-tuple-element.45), channel_id=1, source_target_pairs={{16,0},{32,16},{48,32},{64,48},{80,64},{96,80},{112,96},{128,112},... | collective-permute-start | bytes 368648 | tf_op jit(solution)/shard_map/ppermute | solution.py:25
  123.9 0.3 copy.196
  124.2 0.7 slice.362
  124.9 1.1 copy.193
  126.1 0.2 div.1146
  126.4 0.2 reduce_sum.98
  126.7 4.6 %collective-permute-done.1 = f32[5,3,8,256]{3,2,1,0:T(8,128)} collective-permute-done((f32[5,3,8,256]{3,2,1,0:T(8,128)}, f32[5,3,8,256]{3,2,1,0:T(8,128)}, u32[]{:S(2)}, u32[]{:S(2)}) %collective-permute-start.1) | collective-permute-done | bytes 122912 | tf_op jit(solution)/shard_map/ppermute | solution.py:25
  131.3 1.2 select_select_fusion.1
  132.9 0.8 fusion.133
  134.1 0.7 multiply_reduce_fusion.4
  134.9 0.7 fusion.121
  (81 shorter events, 4.0 us)
Async XLA Ops:
  0.6 5.0 %copy-start.15 = (f32[5]{0:T(128)S(1)}, f32[5]{0:T(128)}, u32[]{:S(2)}) copy-start(f32[5]{0:T(128)} %constant.139) | copy-start | bytes 64
  0.6 5.2 %copy-start.2 = (f32[8,8,256]{2,1,0:T(8,128)S(1)}, f32[8,8,256]{2,1,0:T(8,128)}, u32[]{:S(2)}) copy-start(f32[8,8,256]{2,1,0:T(8,128)} %param.13) | copy-start | bytes 196612
  0.7 5.2 %copy-start.1 = (f32[3,8,8,256]{3,2,1,0:T(8,128)S(1)}, f32[3,8,8,256]{3,2,1,0:T(8,128)}, u32[]{:S(2)}) copy-start(f32[3,8,8,256]{3,2,1,0:T(8,128)} %param.15) | copy-start | bytes 589828
  0.7 5.2 %copy-start.4 = (f32[8,8,256]{2,1,0:T(8,128)S(1)}, f32[8,8,256]{2,1,0:T(8,128)}, u32[]{:S(2)}) copy-start(f32[8,8,256]{2,1,0:T(8,128)} %param.14) | copy-start | bytes 196612
  0.7 2.7 %copy-start.7 = (s32[6]{0:T(128)S(1)}, s32[6]{0:T(128)}, u32[]{:S(2)}) copy-start(s32[6]{0:T(128)} %param.16) | copy-start | bytes 76
  6.1 2.1 %copy-start.13 = (f32[3]{0:T(128)S(1)}, f32[3]{0:T(128)}, u32[]{:S(2)}) copy-start(f32[3]{0:T(128)} %constant.143) | copy-start | bytes 40
  6.1 2.1 %copy-start.14 = (f32[3]{0:T(128)S(1)}, f32[3]{0:T(128)}, u32[]{:S(2)}) copy-start(f32[3]{0:T(128)} %constant.140) | copy-start | bytes 40
  17.3 35.7 %all-to-all-start = ((f32[16,1,5120]{2,1,0:T(1,128)}), f32[16,1,5120]{2,1,0:T(1,128)S(1)}, u32[]{:S(2)}, u32[]{:S(2)}) async-start(f32[16,1,5120]{2,1,0:T(1,128)} %reshape.81), calls=%async_computation | async-start | bytes 655360 | tf_op jit(solution)/shard_map/all_to_all | solution.py:200
  63.4 1.6 %copy-start.12 = (f32[5]{0:T(128)S(1)}, f32[5]{0:T(128)}, u32[]{:S(2)}) copy-start(f32[5]{0:T(128)} %constant.144) | copy-start | bytes 64
  66.2 2.2 %copy-start.10 = (f32[3]{0:T(128)S(1)}, f32[3]{0:T(128)}, u32[]{:S(2)}) copy-start(f32[3]{0:T(128)} %constant.148) | copy-start | bytes 40
  66.2 2.2 %copy-start.11 = (f32[3]{0:T(128)S(1)}, f32[3]{0:T(128)}, u32[]{:S(2)}) copy-start(f32[3]{0:T(128)} %constant.145) | copy-start | bytes 40
  71.6 21.0 %all-to-all-start.1 = ((f32[16,1,5120]{2,1,0:T(1,128)}), f32[16,1,5120]{2,1,0:T(1,128)S(1)}, u32[]{:S(2)}, u32[]{:S(2)}) async-start(f32[16,1,5120]{2,1,0:T(1,128)} %reshape.83), calls=%async_computation.1 | async-start | bytes 655360 | tf_op jit(solution)/shard_map/all_to_all | solution.py:193
  102.7 21.2 %copy-start = (f32[3,8,8,16,16]{4,2,3,1,0:T(8,128)S(1)}, f32[3,8,8,16,16]{4,2,3,1,0:T(8,128)}, u32[]{:S(2)}) copy-start(f32[3,8,8,16,16]{4,2,3,1,0:T(8,128)} %get-tuple-element.27) | copy-start | bytes 589828
  106.2 20.5 %collective-permute-start = (f32[5,3,8,256]{3,2,1,0:T(8,128)}, f32[5,3,8,256]{3,2,1,0:T(8,128)}, u32[]{:S(2)}, u32[]{:S(2)}) collective-permute-start(f32[5,3,8,256]{3,2,1,0:T(8,128)} %get-tuple-element.44), channel_id=1, source_target_pairs={{0,16},{16,32},{32,48},{48,64},{64,80},{80,96},{96,112},{112,128},... | collective-permute-start | bytes 368648 | tf_op jit(solution)/shard_map/ppermute | solution.py:23
  122.0 9.3 %collective-permute-start.1 = (f32[5,3,8,256]{3,2,1,0:T(8,128)}, f32[5,3,8,256]{3,2,1,0:T(8,128)}, u32[]{:S(2)}, u32[]{:S(2)}) collective-permute-start(f32[5,3,8,256]{3,2,1,0:T(8,128)} %get-tuple-element.45), channel_id=1, source_target_pairs={{16,0},{32,16},{48,32},{64,48},{80,64},{96,80},{112,96},{128,112},... | collective-permute-start | bytes 368648 | tf_op jit(solution)/shard_map/ppermute | solution.py:25
  124.2 2.1 %copy-start.3 = (f32[8,8,16,16]{3,1,2,0:T(8,128)S(1)}, f32[8,8,16,16]{3,1,2,0:T(8,128)}, u32[]{:S(2)}) copy-start(f32[8,8,16,16]{3,1,2,0:T(8,128)} %get-tuple-element.26) | copy-start | bytes 196612
  124.2 2.4 %copy-start.5 = (f32[8,8,256]{2,1,0:T(8,128)S(1)}, f32[8,8,256]{2,1,0:T(8,128)}, u32[]{:S(2)}) copy-start(f32[8,8,256]{2,1,0:T(8,128)} %mul.1862) | copy-start | bytes 196612
  124.2 7.1 %copy-start.16 = (f32[5]{0:T(128)S(1)}, f32[5]{0:T(128)}, u32[]{:S(2)}) copy-start(f32[5]{0:T(128)} %constant.149) | copy-start | bytes 64
  132.6 1.3 copy-start.8
  132.6 1.3 copy-start.9
  134.1 1.4 %copy-start.6 = (f32[8,8,256]{2,1,0:T(8,128)}, f32[8,8,256]{2,1,0:T(8,128)S(1)}, u32[]{:S(2)}) copy-start(f32[8,8,256]{2,1,0:T(8,128)S(1)} %fusion.127) | copy-start | bytes 196612
where the time goes:
time: 136 us
  starting transfers between devices  39.1 us (29%)
  waiting for transfers between devices  37.3 us (27%)
  local copies, waits for them, and re-layouts  34.9 us (26%)
  other arithmetic  19.1 us (14%)
  between operations  5.07 us (4%)
    all_to_all x1, starting transfers between devices, on_device(): lax.all_to_all(fields, 'row', split_axis=3, concat_axis=2, tiled=True)  17.7 us
    all_to_all x1, waiting for transfers between devices, on_device(): lax.all_to_all(fields, 'row', split_axis=3, concat_axis=2, tiled=True)  16.7 us
    all_to_all x1, waiting for transfers between devices, return_rows(): lax.all_to_all(fields, 'row', split_axis=2, concat_axis=3, tiled=True)  16 us
    ppermute x1, starting transfers between devices, padded_2(): lax.ppermute(tail, axis, [(i, (i + 1) % count) for i in range(ends)])  15.8 us
    unnamed x40, local copies, waits for them, and re-layouts  12.9 us
    all_to_all x3, local copies, waits for them, and re-layouts, return_rows(): lax.all_to_all(fields, 'row', split_axis=2, concat_axis=3, tiled=True)  6.24 us
    all_to_all x3, local copies, waits for them, and re-layouts, on_device(): lax.all_to_all(fields, 'row', split_axis=3, concat_axis=2, tiled=True)  5.37 us
    ppermute x1, waiting for transfers between devices, padded_2(): lax.ppermute(head, axis, [((i + 1) % count, i) for i in range(ends)])  4.58 us
  transfers between devices with their start and end apart: 4, of which 3 were waited for; matrix products, arithmetic and copies ran while one was open for 2% of the time, Pallas kernels for 0%

commit v1 on v0

--- a/solution.py
+++ b/solution.py
@@ -197,7 +197,12 @@
     fields = jnp.concatenate([density[None], pressure[None], velocity], axis=0)
     fields = sweep_cells(add_ghosts(fields, 3, boundary[0], boundary[1], 2), 3, 2)
     turned = jnp.swapaxes(
-        lax.all_to_all(fields, "row", split_axis=3, concat_axis=2, tiled=True), 2, 3
+        jnp.concatenate(
+            lax.all_to_all(jnp.stack(jnp.split(fields, lax.axis_size("row"), axis=3)), "row", 0, 0),
+            axis=2,
+        ),
+        2,
+        3,
     )
     columns = sweep_cells(add_ghosts(turned, 3, boundary[2], boundary[3], 3), 3, 3)
     fields = z_sweep(return_rows(jnp.swapaxes(columns, 2, 3)), boundary)

time: 136 us -> 129 us (0.949)
  local copies, waits for them, and re-layouts: 34.9 us -> 26.7 us
  other arithmetic: 19.1 us -> 21.7 us
  waiting for transfers between devices: 37.3 us -> 35.4 us
    unnamed x40 -> x53, local copies, waits for them, and re-layouts: 12.9 us -> 7.13 us
    all_to_all x3 -> x1, local copies, waits for them, and re-layouts: 5.37 us -> 0.51 us  [on_device(): lax.all_to_all(jnp.stack(jnp.split(fields, lax.axis_size('row'), axis=3))...]
    reshape x0 -> x2, local copies, waits for them, and re-layouts: none -> 4.3 us  [on_device(): jnp.concatenate(lax.all_to_all(jnp.stack(jnp.split(fields, lax.axis_size(...]
    concatenate x1 -> x0, local copies, waits for them, and re-layouts: 3.1 us -> none  [primitive(): jnp.concatenate([dens, jnp.maximum(press, press_floor), speeds], axis=0)]
    ppermute x1, waiting for transfers between devices: 4.58 us -> 2.73 us  [padded_2(): lax.ppermute(head, axis, [((i + 1) % count, i) for i in range(ends)])]
    add x2, other arithmetic: 0.03 us -> 1.78 us  [conserved(): prims[1:2] / (gamma_gas - 1.0)]
  transfers between devices with their start and end apart: 4 -> 4, of which waited for: 3 -> 3; matrix products, arithmetic and copies ran while one was open for 2% -> 4% of each run, Pallas kernels for 0% -> 0%
where the time goes in v1:
time: 129 us; the launch traced here: 128 us
  starting transfers between devices  39.1 us (30%)
  waiting for transfers between devices  35.4 us (27%)
  local copies, waits for them, and re-layouts  26.7 us (21%)
  other arithmetic  21.7 us (17%)
  between operations  5.27 us (4%)
    all_to_all x1, starting transfers between devices, on_device(): lax.all_to_all(jnp.stack(jnp.split(fields, lax.axis_size('row'), axis=3))...  17.7 us
    all_to_all x1, waiting for transfers between devices, on_device(): lax.all_to_all(jnp.stack(jnp.split(fields, lax.axis_size('row'), axis=3))...  16.7 us
    all_to_all x1, waiting for transfers between devices, return_rows(): lax.all_to_all(fields, 'row', split_axis=2, concat_axis=3, tiled=True)  15.9 us
    ppermute x1, starting transfers between devices, padded_2(): lax.ppermute(tail, axis, [(i, (i + 1) % count) for i in range(ends)])  15.8 us
    unnamed x53, local copies, waits for them, and re-layouts  7.13 us
    all_to_all x3, local copies, waits for them, and re-layouts, return_rows(): lax.all_to_all(fields, 'row', split_axis=2, concat_axis=3, tiled=True)  6.21 us
    reshape x2, local copies, waits for them, and re-layouts, on_device(): jnp.concatenate(lax.all_to_all(jnp.stack(jnp.split(fields, lax.axis_size(...  4.3 us
    all_to_all x1, starting transfers between devices, return_rows(): lax.all_to_all(fields, 'row', split_axis=2, concat_axis=3, tiled=True)  3.76 us
  transfers between devices with their start and end apart: 4, of which 3 were waited for; matrix products, arithmetic and copies ran while one was open for 4% of the time, Pallas kernels for 0%

profile of v1, /device:TPU:24, one launch (start us, length us, event | category | flops | bytes accessed | tf_op | source)
XLA Modules:
  0.0 128.1 jit_solution(12283913471412901532)
XLA Ops:
  0.7 1.0 multiply_reduce_fusion.8
  1.7 1.0 fusion.16
  2.9 1.5 %fusion.160 = (s32[1]{0:T(128)}, s32[1]{0:T(128)}, s32[1]{0:T(128)}, s32[1]{0:T(128)}, s32[1]{0:T(128)}, /*index=5*/s32[1]{0:T(128)}) fusion(s32[6]{0:T(128)} %param.16), kind=kLoop, calls=%fused_computation.315 | loop fusion | bytes 48 | tf_op jit(solution)/shard_map/slice | solution.py:188
  5.7 0.9 add_bitcast_fusion
  6.6 0.3 copy.167
  7.0 0.3 copy.168
  7.9 0.5 fusion.7
  8.4 0.3 minimum_add_fusion.3
  8.7 1.2 fusion.148
  12.3 1.7 %reshape.89 = f32[16,1,5120]{2,1,0:T(1,128)} reshape(f32[16,5,8,8,16]{4,3,2,1,0:T(8,128)S(1)} %fusion.26) | data formatting | bytes 655360
  14.0 17.7 %all-to-all-start = ((f32[16,1,5120]{2,1,0:T(1,128)}), f32[16,1,5120]{2,1,0:T(1,128)S(1)}, u32[]{:S(2)}, u32[]{:S(2)}) async-start(f32[16,1,5120]{2,1,0:T(1,128)} %reshape.89), calls=%async_computation | async-start | bytes 655360 | tf_op jit(solution)/shard_map/all_to_all | solution.py:201
  32.9 16.7 %all-to-all-done = f32[16,1,5120]{2,1,0:T(1,128)S(1)} async-done(((f32[16,1,5120]{2,1,0:T(1,128)}), f32[16,1,5120]{2,1,0:T(1,128)S(1)}, u32[]{:S(2)}, u32[]{:S(2)}) %all-to-all-start) | async-done | bytes 327712 | tf_op jit(solution)/shard_map/all_to_all | solution.py:201
  49.6 0.5 broadcast.1082
  50.1 1.4 %reduce.5 = f32[16,5120]{1,0:T(8,128)S(1)} reduce(f32[16,1,5120]{2,1,0:T(1,128)S(1)} %all-to-all-done, f32[]{:T(128)} %broadcast.1082), dimensions={1}, to_apply=%all_to_all.16.reduce_sub_computation | reduce | bytes 655364 | tf_op jit(solution)/shard_map/all_to_all | solution.py:201
  51.6 0.9 reshape.90
  52.5 1.9 %copy_bitcast_fusion.1 = f32[5,8,128,16]{3,2,1,0:T(8,128)} fusion(f32[16,5,8,8,16]{4,3,2,1,0:T(8,128)S(1)} %reshape.90), kind=kLoop, calls=%fused_computation.1 | loop fusion | bytes 655360 | tf_op jit(solution)/shard_map/reshape | solution.py:200
  54.3 2.4 %copy.157 = f32[5,8,128,16]{2,3,1,0:T(8,128)S(1)} copy(f32[5,8,128,16]{3,2,1,0:T(8,128)} %copy_bitcast_fusion.1) | data formatting | bytes 655360 | tf_op jit(solution)/shard_map/reshape | solution.py:200
  56.8 0.4 slice_reduce_fusion.1
  57.9 0.3 pad_maximum_fusion
  58.3 0.6 fusion.3
  58.9 0.4 minimum_add_fusion.1
  59.3 1.6 %fusion.147 = (pred[8,16,129]{2,1,0:T(8,128)(4,1)S(1)}, f32[1,8,16,129]{3,2,1,0:T(8,128)S(1)}, f32[1,8,16,129]{3,2,1,0:T(8,128)S(1)}) fusion(f32[5,8,16,130]{3,2,1,0:T(8,128)S(1)} %get-tuple-element.33, f32[5,8,16,130]{3,2,1,0:T(8,128)S(1)} %get-tuple-element.32), kind=kLoop, calls=%fused_computation.304 | loop fusion | flops 2889600 | bytes 544896 | tf_op jit(solution)/shard_map/jit(_where)/broadcast_in_dim | solution.py:145
  61.7 0.8 copy.158
  62.6 1.7 %reshape.91 = f32[16,1,5120]{2,1,0:T(1,128)} reshape(f32[128,5,8,16]{3,2,1,0:T(8,128)S(1)} %bitcast.184) | data formatting | bytes 655360
  64.3 3.8 %all-to-all-start.1 = ((f32[16,1,5120]{2,1,0:T(1,128)}), f32[16,1,5120]{2,1,0:T(1,128)S(1)}, u32[]{:S(2)}, u32[]{:S(2)}) async-start(f32[16,1,5120]{2,1,0:T(1,128)} %reshape.91), calls=%async_computation.1 | async-start | bytes 655360 | tf_op jit(solution)/shard_map/all_to_all | solution.py:193
  69.3 15.9 %all-to-all-done.1 = f32[16,1,5120]{2,1,0:T(1,128)S(1)} async-done(((f32[16,1,5120]{2,1,0:T(1,128)}), f32[16,1,5120]{2,1,0:T(1,128)S(1)}, u32[]{:S(2)}, u32[]{:S(2)}) %all-to-all-start.1) | async-done | bytes 327712 | tf_op jit(solution)/shard_map/all_to_all | solution.py:193
  85.2 1.4 %reduce.6 = f32[16,5120]{1,0:T(8,128)S(1)} reduce(f32[16,1,5120]{2,1,0:T(1,128)S(1)} %all-to-all-done.1, f32[]{:T(128)} %broadcast.1082), dimensions={1}, to_apply=%all_to_all.17.reduce_sub_computation | reduce | bytes 655364 | tf_op jit(solution)/shard_map/all_to_all | solution.py:193
  86.7 0.9 reshape.92
  87.5 0.5 copy.171
  88.0 0.9 slice_multiply_fusion
  88.9 2.2 %multiply_reduce_fusion = (f32[8,8,16,16]{3,1,2,0:T(8,128)}, f32[3,8,8,16,16]{4,2,3,1,0:T(8,128)}) fusion(f32[5,8,8,16,16]{4,2,3,1,0:T(8,128)S(1)} %bitcast.183), kind=kLoop, calls=%fused_computation.2 | loop fusion | flops 81920 | bytes 458752 | tf_op jit(solution)/shard_map/reduce_sum | solution.py:90
  91.5 0.9 mul.1862
  92.3 3.0 %copy.165 = f32[5,8,8,16,16]{4,3,2,1,0:T(8,128)} copy(f32[5,8,8,16,16]{4,1,0,2,3:T(8,128)S(1)} %bitcast.181) | data formatting | bytes 655360 | tf_op jit(solution)/shard_map/all_to_all | solution.py:193
  95.4 2.7 %all_to_all.20 = f32[5,8,8,256]{3,2,1,0:T(8,128)S(1)} reshape(f32[5,8,8,16,16]{4,3,2,1,0:T(8,128)} %copy.165) | data formatting | bytes 655360 | tf_op jit(solution)/shard_map/all_to_all | solution.py:193
  98.1 0.7 fusion.155
  98.8 15.8 %collective-permute-start = (f32[5,3,8,256]{3,2,1,0:T(8,128)}, f32[5,3,8,256]{3,2,1,0:T(8,128)}, u32[]{:S(2)}, u32[]{:S(2)}) collective-permute-start(f32[5,3,8,256]{3,2,1,0:T(8,128)} %get-tuple-element.44), channel_id=1, source_target_pairs={{0,16},{16,32},{32,48},{48,64},{64,80},{80,96},{96,112},{112,128},... | collective-permute-start | bytes 368648 | tf_op jit(solution)/shard_map/ppermute | solution.py:23
  114.6 1.9 %collective-permute-start.1 = (f32[5,3,8,256]{3,2,1,0:T(8,128)}, f32[5,3,8,256]{3,2,1,0:T(8,128)}, u32[]{:S(2)}, u32[]{:S(2)}) collective-permute-start(f32[5,3,8,256]{3,2,1,0:T(8,128)} %get-tuple-element.45), channel_id=1, source_target_pairs={{16,0},{32,16},{48,32},{64,48},{80,64},{96,80},{112,96},{128,112},... | collective-permute-start | bytes 368648 | tf_op jit(solution)/shard_map/ppermute | solution.py:25
  116.6 0.9 reduce_sum.98
  117.6 0.9 div.1146
  118.4 0.3 copy.164
  118.7 0.7 slice.362
  119.4 0.9 broadcast_multiply_fusion
  120.3 0.9 multiply_add_fusion.3
  121.2 2.7 %collective-permute-done.1 = f32[5,3,8,256]{3,2,1,0:T(8,128)} collective-permute-done((f32[5,3,8,256]{3,2,1,0:T(8,128)}, f32[5,3,8,256]{3,2,1,0:T(8,128)}, u32[]{:S(2)}, u32[]{:S(2)}) %collective-permute-start.1) | collective-permute-done | bytes 122912 | tf_op jit(solution)/shard_map/ppermute | solution.py:25
  123.9 1.2 select_select_fusion.1
  125.5 0.8 fusion.149
  126.7 0.7 multiply_reduce_fusion.4
  127.4 0.6 fusion.137
  (94 shorter events, 5.8 us)
Async XLA Ops:
  0.6 6.8 %copy-start.14 = (f32[5]{0:T(128)S(1)}, f32[5]{0:T(128)}, u32[]{:S(2)}) copy-start(f32[5]{0:T(128)} %constant.139) | copy-start | bytes 64
  0.6 7.0 %copy-start.1 = (f32[3,8,8,256]{3,2,1,0:T(8,128)S(1)}, f32[3,8,8,256]{3,2,1,0:T(8,128)}, u32[]{:S(2)}) copy-start(f32[3,8,8,256]{3,2,1,0:T(8,128)} %param.15) | copy-start | bytes 589828
  0.7 7.0 %copy-start.2 = (f32[8,8,256]{2,1,0:T(8,128)S(1)}, f32[8,8,256]{2,1,0:T(8,128)}, u32[]{:S(2)}) copy-start(f32[8,8,256]{2,1,0:T(8,128)} %param.13) | copy-start | bytes 196612
  0.7 7.0 %copy-start.5 = (f32[8,8,256]{2,1,0:T(8,128)S(1)}, f32[8,8,256]{2,1,0:T(8,128)}, u32[]{:S(2)}) copy-start(f32[8,8,256]{2,1,0:T(8,128)} %param.14) | copy-start | bytes 196612
  7.9 2.1 %copy-start.12 = (f32[3]{0:T(128)S(1)}, f32[3]{0:T(128)}, u32[]{:S(2)}) copy-start(f32[3]{0:T(128)} %constant.143) | copy-start | bytes 40
  7.9 2.1 %copy-start.13 = (f32[3]{0:T(128)S(1)}, f32[3]{0:T(128)}, u32[]{:S(2)}) copy-start(f32[3]{0:T(128)} %constant.140) | copy-start | bytes 40
  14.0 35.7 %all-to-all-start = ((f32[16,1,5120]{2,1,0:T(1,128)}), f32[16,1,5120]{2,1,0:T(1,128)S(1)}, u32[]{:S(2)}, u32[]{:S(2)}) async-start(f32[16,1,5120]{2,1,0:T(1,128)} %reshape.89), calls=%async_computation | async-start | bytes 655360 | tf_op jit(solution)/shard_map/all_to_all | solution.py:201
  56.8 0.9 copy-start.11
  58.9 2.2 %copy-start.9 = (f32[3]{0:T(128)S(1)}, f32[3]{0:T(128)}, u32[]{:S(2)}) copy-start(f32[3]{0:T(128)} %constant.148) | copy-start | bytes 40
  58.9 2.2 %copy-start.10 = (f32[3]{0:T(128)S(1)}, f32[3]{0:T(128)}, u32[]{:S(2)}) copy-start(f32[3]{0:T(128)} %constant.145) | copy-start | bytes 40
  64.3 21.0 %all-to-all-start.1 = ((f32[16,1,5120]{2,1,0:T(1,128)}), f32[16,1,5120]{2,1,0:T(1,128)S(1)}, u32[]{:S(2)}, u32[]{:S(2)}) async-start(f32[16,1,5120]{2,1,0:T(1,128)} %reshape.91), calls=%async_computation.1 | async-start | bytes 655360 | tf_op jit(solution)/shard_map/all_to_all | solution.py:193
  95.4 21.2 %copy-start.3 = (f32[8,8,16,16]{3,1,2,0:T(8,128)S(1)}, f32[8,8,16,16]{3,1,2,0:T(8,128)}, u32[]{:S(2)}) copy-start(f32[8,8,16,16]{3,1,2,0:T(8,128)} %get-tuple-element.26) | copy-start | bytes 196612
  95.4 22.1 %copy-start.4 = (f32[1,8,8,16,16]{4,2,3,1,0:T(8,128)S(1)}, f32[1,8,8,16,16]{4,2,3,1,0:T(8,128)}, u32[]{:S(2)}) copy-start(f32[1,8,8,16,16]{4,2,3,1,0:T(8,128)} %get-tuple-element.28) | copy-start | bytes 196612
  98.1 20.4 %copy-start = (f32[3,8,8,16,16]{4,2,3,1,0:T(8,128)S(1)}, f32[3,8,8,16,16]{4,2,3,1,0:T(8,128)}, u32[]{:S(2)}) copy-start(f32[3,8,8,16,16]{4,2,3,1,0:T(8,128)} %get-tuple-element.27) | copy-start | bytes 589828
  98.8 22.4 %collective-permute-start = (f32[5,3,8,256]{3,2,1,0:T(8,128)}, f32[5,3,8,256]{3,2,1,0:T(8,128)}, u32[]{:S(2)}, u32[]{:S(2)}) collective-permute-start(f32[5,3,8,256]{3,2,1,0:T(8,128)} %get-tuple-element.44), channel_id=1, source_target_pairs={{0,16},{16,32},{32,48},{48,64},{64,80},{80,96},{96,112},{112,128},... | collective-permute-start | bytes 368648 | tf_op jit(solution)/shard_map/ppermute | solution.py:23
  114.6 9.3 %collective-permute-start.1 = (f32[5,3,8,256]{3,2,1,0:T(8,128)}, f32[5,3,8,256]{3,2,1,0:T(8,128)}, u32[]{:S(2)}, u32[]{:S(2)}) collective-permute-start(f32[5,3,8,256]{3,2,1,0:T(8,128)} %get-tuple-element.45), channel_id=1, source_target_pairs={{16,0},{32,16},{48,32},{64,48},{80,64},{96,80},{112,96},{128,112},... | collective-permute-start | bytes 368648 | tf_op jit(solution)/shard_map/ppermute | solution.py:25
  118.4 5.5 %copy-start.15 = (f32[5]{0:T(128)S(1)}, f32[5]{0:T(128)}, u32[]{:S(2)}) copy-start(f32[5]{0:T(128)} %constant.149) | copy-start | bytes 64
  125.2 1.2 copy-start.7
  125.2 1.2 copy-start.8
  126.7 1.4 %copy-start.6 = (f32[8,8,256]{2,1,0:T(8,128)}, f32[8,8,256]{2,1,0:T(8,128)S(1)}, u32[]{:S(2)}) copy-start(f32[8,8,256]{2,1,0:T(8,128)S(1)} %fusion.143) | copy-start | bytes 196612
